TPU v7x, 256 devices: a whole 4x4x8 slice. The times are simulated.
256 devices in a mesh: bl: 32 (over x, z), ta: 8 (over y, core).
Axes of the slice: x: 4, y: 4, z: 8, core: 2. Of those that a mesh axis runs over, the one named last changes fastest.
Arguments:
- log_amplitude: bfloat16 [8192, 8, 1536], P('bl', 'ta'), may hold values from -2.5 to 2.5
- phase: bfloat16 [8192, 8, 1536], P('bl', 'ta'), may hold values from -4 to 4
- redundant_group_index: int32 [8192], P('bl'), may hold values from 0 to 223, as said below
- antenna_couples: int32 [8192, 2], P('bl'), may hold values from 0 to 349, as said below
- tile_flag_mask: int32 [8192, 12], P(('bl', 'ta')), may hold values from 0 to 1, as said below
- inverse: float32 [2, 350, 350], replicated, may hold values from -1 to 1
- integration_kernel: float32 [8, 8], replicated, may hold values from 0.01 to 1
- channel_kernel: bfloat16 [7, 128, 128], replicated, may hold values from 0.0009994507 to 1
Outputs:
- antenna_gains: float32 [2, 350, 8, 1536], P(None, None, 'ta')
- filled: float32 [2, 8192, 8, 1536], P(None, ('bl', 'ta'))
Inputs may be any that keep to these rules, and one draw needn't show every extreme that they name: `redundant_group_index`: every group from 0 to 223 holds at least one baseline. `antenna_couples`: the two antennas of a baseline differ. `tile_flag_mask`: both neighbouring tiles of a flagged tile are unflagged.
All inputs are finite; a program needn't handle non-finite values.
Results may differ from a plain program's by a relative error of at most 0.0029.
Values may be sent and summed in bfloat16 or wider, within the bound.
A program may use at most 64 MiB of HBM per device.

v0:
```python
import jax
import jax.numpy as jnp
from jax import lax
from jax.sharding import PartitionSpec as P

ANTENNA_COUNT = 350
NGRP = 224


def mix_channels(values, channel_kernel):
    span_tiles = (channel_kernel.shape[0] - 1) // 2
    tile_width = channel_kernel.shape[1]
    leading = values.shape[:-1]
    tile_count = values.shape[-1] // tile_width
    tiled = values.reshape(leading + (tile_count, tile_width))
    pad_spec = [(0, 0)] * len(leading) + [(span_tiles, span_tiles), (0, 0)]
    padded = jnp.pad(tiled, pad_spec)
    summed = jnp.zeros(leading + (tile_count, tile_width), jnp.float32)
    for offset in range(2 * span_tiles + 1):
        window = lax.slice_in_dim(padded, offset, offset + tile_count, axis=len(leading))
        summed = summed + jnp.einsum(
            "...kj,ij->...ki", window, channel_kernel[offset], preferred_element_type=jnp.float32
        )
    return summed.reshape(leading + (tile_count * tile_width,))


def fill_block(calibrated, tile_flag_mask, integration_kernel, channel_kernel):
    tile_width = channel_kernel.shape[1]
    weight = jnp.repeat((1 - tile_flag_mask).astype(jnp.bfloat16), tile_width, axis=1)
    masked = calibrated * weight[None, :, None, :]
    mixed = mix_channels(masked, channel_kernel)
    numerator = jnp.einsum(
        "tu,kbuf->kbtf", integration_kernel, mixed, precision=lax.Precision.HIGHEST
    )
    weight_mix = mix_channels(weight, channel_kernel)
    denominator = jnp.sum(integration_kernel, axis=1)[None, :, None] * weight_mix[:, None, :]
    keep = weight.astype(jnp.float32)[None, :, None, :]
    return keep * calibrated.astype(jnp.float32) + (1.0 - keep) * numerator / denominator[None]


def solve_columns(inverse, normal_right_side):
    return jnp.einsum("sab,sbtf->satf", inverse, normal_right_side, precision=lax.Precision.HIGHEST)


def on_device(
    log_amplitude,
    phase,
    redundant_group_index,
    antenna_couples,
    tile_flag_mask,
    inverse,
    integration_kernel,
    channel_kernel,
):
    stacked_terms = jnp.stack([log_amplitude, phase])
    first_antenna = antenna_couples[:, 0]
    second_antenna = antenna_couples[:, 1]
    group_hot = (
        redundant_group_index[:, None] == jnp.arange(NGRP, dtype=jnp.int32)[None, :]
    ).astype(jnp.bfloat16)
    antenna_labels = jnp.arange(ANTENNA_COUNT, dtype=jnp.int32)[None, :]
    first_onehot = (first_antenna[:, None] == antenna_labels).astype(jnp.float32)
    second_onehot = (second_antenna[:, None] == antenna_labels).astype(jnp.float32)
    signed_float = jnp.stack([first_onehot + second_onehot, first_onehot - second_onehot])
    group_part = jnp.einsum(
        "bg,sbtf->sgtf", group_hot, stacked_terms, preferred_element_type=jnp.float32
    )
    count_part = jnp.sum(group_hot.astype(jnp.float32), axis=0)
    group_sums, group_counts = lax.psum((group_part, count_part), "bl")
    group_mean = group_sums / group_counts[None, :, None, None]
    fit_residual = stacked_terms.astype(jnp.float32) - jnp.take(
        group_mean, redundant_group_index, axis=1
    )
    rhs_part = jnp.einsum(
        "sba,sbtf->satf", signed_float, fit_residual, precision=lax.Precision.HIGHEST
    )
    normal_right_side = lax.psum(rhs_part, "bl")
    antenna_gains = solve_columns(inverse, normal_right_side)
    amplitude_gain = antenna_gains[0]
    phase_gain_term = antenna_gains[1]
    calibrated_amplitude = (
        log_amplitude.astype(jnp.float32)
        - jnp.take(amplitude_gain, first_antenna, axis=0)
        - jnp.take(amplitude_gain, second_antenna, axis=0)
    )
    calibrated_phase = (
        phase.astype(jnp.float32)
        - jnp.take(phase_gain_term, first_antenna, axis=0)
        + jnp.take(phase_gain_term, second_antenna, axis=0)
    )
    magnitude = jnp.exp(calibrated_amplitude)
    calibrated = jnp.stack(
        [magnitude * jnp.cos(calibrated_phase), magnitude * jnp.sin(calibrated_phase)]
    ).astype(jnp.bfloat16)
    filled = fill_block(
        lax.all_to_all(calibrated, "ta", split_axis=1, concat_axis=2, tiled=True),
        tile_flag_mask,
        integration_kernel,
        channel_kernel,
    )
    return (antenna_gains, filled)


def solution(mesh):
    in_specs = (
        P("bl", "ta", None),
        P("bl", "ta", None),
        P("bl"),
        P("bl", None),
        P(("bl", "ta"), None),
        P(),
        P(),
        P(),
    )
    out_specs = (P(None, None, "ta", None), P(None, ("bl", "ta"), None, None))
    return jax.shard_map(
        on_device, mesh=mesh, in_specs=in_specs, out_specs=out_specs, check_vma=False
    )
```

profile of v0, /device:TPU:1, one launch (start us, length us, event | category | flops | bytes accessed | tf_op | source)
XLA Modules:
  0.0 452.8 jit_solution(7222060183240848524)
XLA Ops:
  7.2 0.0 all-reduce.5.cloned.1.call-start
  7.2 3.5 convolution_bitcast_fusion
  10.8 0.0 all-reduce.5.cloned.1.call-update
  10.8 0.0 all-reduce.7.cloned.1.call-start
  10.8 0.6 copy-done.10
  11.4 0.1 convert_reduce_fusion
  11.5 64.8 %psum.22 = f32[224]{0:T(256)S(1)} all-reduce(f32[224]{0:T(256)S(1)} %convert_reduce_fusion), channel_id=1, replica_groups=mesh['bl'=32,'ta'=8] {'bl'}, use_global_device_ids=true, to_apply=%region_2.0 | all-reduce | flops 224 | bytes 1792 | tf_op jit(solution)/shard_map/psum | solution.py:69
  76.4 0.1 convert_add_fusion
  76.4 92.5 %all-reduce.5.cloned.1.call-done = f32[2,224,1,1536]{3,1,0,2:T(8,128)} async-done(((f32[2,224,1,1536]{3,1,0,2:T(8,128)}), f32[2,224,1,1536]{3,1,0,2:T(8,128)}) %all-reduce.5.cloned.1.call-update) | async-done | bytes 2752528 | tf_op jit(solution)/shard_map/psum | solution.py:69
  169.0 2.1 divide_bitcast_fusion
  171.0 3.7 copy.54
  174.7 7.3 %gather_fusion = f32[256,2,1536]{2,1,0:T(2,128)} fusion(f32[2,224,1536]{2,0,1:T(2,128)} %copy.54, s32[1024]{0:T(1024)S(1)} %pad_clamp_fusion.2), kind=kCustom, calls=%fused_computation.4 | custom fusion | bytes 6292480 | tf_op jit(solution)/shard_map/jit(_take)/gather | solution.py:71
  182.0 8.8 %fusion.3 = f32[2,350,1536]{2,1,0:T(8,128)} fusion(f32[256,2,1536]{2,1,0:T(2,128)} %gather_fusion, bf16[1,256,1536]{2,1,0:T(8,128)(2,1)S(1)} %bitcast.201, bf16[1,256,1536]{2,1,0:T(8,128)(2,1)S(1)} %bitcast.203, pred[256]{0:T(512)(128)(4,1)S(1)} %compare_and_fusion.2, f32[1,256,350]{1,2,0:T(8,128)S(1)} %get-tuple-element.22, ...), kind=kOutput, calls=%fused_computation.11 | convolution fusion | flops 3306339328 | bytes 9736448 | tf_op jit(solution)/shard_map/sba,sbtf->satf/dot_general | solution.py:74
  190.9 0.7 copy-done.11
  191.5 0.1 copy.74
  191.6 0.1 copy-done.7
  191.8 0.2 fusion.45
  192.0 0.2 convolution_add_fusion.4
  192.2 0.2 convolution_add_fusion.3
  192.5 0.2 convolution_add_fusion.5
  192.7 0.2 convolution_add_fusion.2
  193.0 0.2 convolution_add_fusion.1
  193.2 0.2 fusion.28
  193.5 0.1 reduce_sum.19
  193.6 160.5 %all-reduce.7.cloned.1.call-done = f32[2,350,1536]{2,1,0:T(8,128)} async-done(((f32[2,350,1536]{2,1,0:T(8,128)}), f32[2,350,1536]{2,1,0:T(8,128)}) %all-reduce.7.cloned.1.call-update) | async-done | bytes 4300816 | tf_op jit(solution)/shard_map/psum | solution.py:77
  354.1 9.4 %fusion.29 = f32[2,1536,350]{1,2,0:T(8,128)S(1)} fusion(f32[2,350,1536]{2,1,0:T(8,128)} %all-reduce.7.cloned.1.call-done, f32[2,350,350]{2,0,1:T(2,128)S(1)} %copy-done), kind=kOutput, calls=%fused_computation.56 | convolution fusion | flops 4515840000 | bytes 9581600 | tf_op jit(solution)/shard_map/sab,sbtf->satf/dot_general | solution.py:42
  363.5 1.8 slice_bitcast_fusion.1
  365.4 0.8 copy-done.2
  366.2 4.7 %gather_fusion.2 = f32[256,1536]{1,0:T(8,128)} fusion(f32[350,1536]{1,0:T(8,128)} %get-tuple-element.19, s32[1024]{0:T(1024)S(1)} %pad_clamp_fusion), kind=kCustom, calls=%fused_computation.1.clone | custom fusion | bytes 3146752 | tf_op jit(solution)/shard_map/jit(_take)/gather | solution.py:84
  370.9 4.7 %gather_fusion.1 = f32[256,1536]{1,0:T(8,128)} fusion(f32[350,1536]{1,0:T(8,128)} %get-tuple-element.19, s32[1024]{0:T(1024)S(1)} %pad_clamp_fusion.1), kind=kCustom, calls=%fused_computation.clone | custom fusion | bytes 3146752 | tf_op jit(solution)/shard_map/jit(_take)/gather | solution.py:83
  375.7 2.3 gather_fusion.3
  378.0 2.3 gather_fusion.4
  380.3 9.3 %fusion.31 = (bf16[1,256,1,1536]{3,1,2,0:T(8,128)(2,1)S(1)}, bf16[1,256,1,1536]{3,1,2,0:T(8,128)(2,1)S(1)}) fusion(f32[256,1536]{1,0:T(8,128)} %gather_fusion.4, pred[256]{0:T(512)(128)(4,1)S(1)} %get-tuple-element.25, f32[256,1536]{1,0:T(8,128)} %gather_fusion.3, pred[256]{0:T(512)(128)(4,1)S(1)} %get-tuple-element.26, ...), kind=kLoop, calls=%fused_computation.58 | loop fusion | flops 5505024 | bytes 9437696 | tf_op jit(solution)/shard_map/stack | solution.py:92
  389.7 0.1 pad_maximum_fusion
  389.8 2.8 copy.58
  392.6 7.5 %all-to-all-start = ((bf16[2,256,1,1536]{3,0,2,1:T(2,128)(2,1)}), bf16[2,256,1,1536]{3,0,2,1:T(2,128)(2,1)S(1)}, u32[]{:S(2)}, u32[]{:S(2)}) async-start(bf16[2,256,1,1536]{3,0,2,1:T(2,128)(2,1)} %copy.58), calls=%async_computation | async-start | bytes 3145728 | tf_op jit(solution)/shard_map/all_to_all | solution.py:96
  400.1 0.1 broadcast_in_dim.34.clone
  400.3 1.4 broadcast_multiply_fusion
  401.7 8.7 %copy.63 = f32[2,350,1,1536]{3,2,1,0:T(1,128)} copy(f32[2,350,1,1536]{3,1,0,2:T(8,128)} %bitcast.199) | data formatting | bytes 8601600
  410.5 10.2 %all-to-all-done = bf16[2,256,1,1536]{3,0,2,1:T(2,128)(2,1)S(1)} async-done(((bf16[2,256,1,1536]{3,0,2,1:T(2,128)(2,1)}), bf16[2,256,1,1536]{3,0,2,1:T(2,128)(2,1)S(1)}, u32[]{:S(2)}, u32[]{:S(2)}) %all-to-all-start) | async-done | bytes 1572896 | tf_op jit(solution)/shard_map/all_to_all | solution.py:96
  420.7 1.1 fusion.18
  421.8 1.1 fusion.60
  422.9 1.2 fusion.58
  424.0 1.2 fusion.56
  425.3 2.9 fusion.53
  428.2 2.9 fusion.51
  431.1 2.9 fusion.49
  434.0 11.8 %fusion.1 = f32[2,32,8,1536]{3,2,1,0:T(8,128)} fusion(f32[2,32,8,12,128]{4,2,3,1,0:T(8,128)} %fusion.49, f32[2,32,8,12,128]{4,2,3,1,0:T(8,128)} %fusion.51, f32[2,32,8,12,128]{4,2,3,1,0:T(8,128)} %fusion.53, f32[2,32,8,12,128]{4,2,3,1,0:T(8,128)S(1)} %fusion.18, f32[2,32,8,12,128]{4,2,3,1,0:T(8,128)S(1)} %fusion.56, f32[2,32,8,12,128]{4,2,3,1,0:T(8,128)S(1)} %fusion.60, ...), kind=kOutput, calls=%fused_computation.8 | convolution fusion | flops 84148224 | bytes 28705024 | tf_op jit(solution)/shard_map/tu,kbuf->kbtf/dot_general | solution.py:32
  (36 shorter events, 0.2 us)
Async XLA Ops:
  7.2 347.0 %copy-start = (f32[2,350,350]{2,0,1:T(2,128)S(1)}, f32[2,350,350]{2,0,1:T(2,128)}, u32[]{:S(2)}) copy-start(f32[2,350,350]{2,0,1:T(2,128)} %param.15) | copy-start | bytes 2940004
  7.2 161.8 %all-reduce.5.cloned.1.call-start = ((), (), s32[]{:S(2)}) async-start(), calls=%async_computation.1 | async-start | bytes 5505024 | tf_op jit(solution)/shard_map/psum | solution.py:69
  10.7 0.7 copy-start.10
  10.7 65.6 %copy-start.12 = (s32[256,2]{0,1:T(2,128)S(1)}, s32[256,2]{0,1:T(2,128)}, u32[]{:S(2)}) copy-start(s32[256,2]{0,1:T(2,128)} %param.13) | copy-start | bytes 6148
  10.8 343.4 %all-reduce.7.cloned.1.call-start = ((), (), s32[]{:S(2)}) async-start(), calls=%async_computation.2 | async-start | bytes 8650752 | tf_op jit(solution)/shard_map/psum | solution.py:77
  174.7 7.3 %copy-start.4 = (bf16[256,1,1536]{2,0,1:T(8,128)(2,1)S(1)}, bf16[256,1,1536]{2,0,1:T(8,128)(2,1)}, u32[]{:S(2)}) copy-start(bf16[256,1,1536]{2,0,1:T(8,128)(2,1)} %param.11) | copy-start | bytes 2359300
  174.7 7.3 %copy-start.6 = (bf16[256,1,1536]{2,0,1:T(8,128)(2,1)S(1)}, bf16[256,1,1536]{2,0,1:T(8,128)(2,1)}, u32[]{:S(2)}) copy-start(bf16[256,1,1536]{2,0,1:T(8,128)(2,1)} %param.10) | copy-start | bytes 2359300
  190.8 0.7 copy-start.11
  190.8 1.0 copy-start.7
  191.8 1.7 copy-start.9
  363.5 2.7 copy-start.2
  378.0 2.3 copy-start.5
  392.6 28.1 %all-to-all-start = ((bf16[2,256,1,1536]{3,0,2,1:T(2,128)(2,1)}), bf16[2,256,1,1536]{3,0,2,1:T(2,128)(2,1)S(1)}, u32[]{:S(2)}, u32[]{:S(2)}) async-start(bf16[2,256,1,1536]{3,0,2,1:T(2,128)(2,1)} %copy.58), calls=%async_computation | async-start | bytes 3145728 | tf_op jit(solution)/shard_map/all_to_all | solution.py:96
  401.7 19.0 %copy-start.8 = (bf16[7,128,128]{2,1,0:T(8,128)(2,1)S(1)}, bf16[7,128,128]{2,1,0:T(8,128)(2,1)}, u32[]{:S(2)}) copy-start(bf16[7,128,128]{2,1,0:T(8,128)(2,1)} %param.17) | copy-start | bytes 688132
  431.0 2.9 copy-start.3
  434.0 11.8 %copy-start.1 = (f32[2,350,350]{2,0,1:T(2,128)S(1)}, f32[2,350,350]{2,0,1:T(2,128)}, u32[]{:S(2)}) copy-start(f32[2,350,350]{2,0,1:T(2,128)} %param.15) | copy-start | bytes 2940004
Sparse Core Ops, SparseCore 0:
  12.1 156.7 all-reduce.4
  191.0 163.1 all-reduce.6
where the time goes:
time: 461 us; the launch traced here: 453 us
  waiting for transfers between devices  263 us (57%)
  blocking collectives  64.8 us (14%)
  matrix products  48.4 us (10%)
  local copies, waits for them, and re-layouts  41 us (9%)
  between operations  14.5 us (3%)
  other arithmetic  13.4 us (3%)
  starting transfers between devices  7.6 us (2%)
    psum x1, waiting for transfers between devices, on_device(): normal_right_side = lax.psum(rhs_part, 'bl')  161 us
    psum x1, waiting for transfers between devices, on_device(): group_sums, group_counts = lax.psum((group_part, count_part), 'bl')  92.5 us
    psum x1, blocking collectives, on_device(): group_sums, group_counts = lax.psum((group_part, count_part), 'bl')  64.8 us
    dot_general x14, matrix products, mix_channels(): jnp.einsum('...kj,ij->...ki', window, channel_kernel[offset], preferred_e...  14.9 us
    dot_general x1, matrix products, fill_block(): jnp.einsum('tu,kbuf->kbtf', integration_kernel, mixed, precision=lax.Prec...  11.8 us
    unnamed x28, local copies, waits for them, and re-layouts  11.1 us
    all_to_all x1, waiting for transfers between devices, on_device(): lax.all_to_all(calibrated, 'ta', split_axis=1, concat_axis=2, tiled=True)  10.2 us
    another operation x2, other arithmetic, on_device(): jnp.stack([magnitude * jnp.cos(calibrated_phase), magnitude * jnp.sin(cal...  9.48 us
  transfers between devices with their start and end apart: 3, of which 3 were waited for; matrix products, arithmetic and copies ran while one was open for 3% of the time, Pallas kernels for 0%

commit v1 on v0

--- a/solution.py
+++ b/solution.py
@@ -74,7 +74,10 @@
     rhs_part = jnp.einsum(
         "sba,sbtf->satf", signed_float, fit_residual, precision=lax.Precision.HIGHEST
     )
-    normal_right_side = lax.psum(rhs_part, "bl")
+    size, normal_right_side = (lax.axis_size("bl"), rhs_part)
+    for reach in [1 << k for k in range(size.bit_length() - 1)]:
+        swap = [(i, i ^ reach) for i in range(size)]
+        normal_right_side = normal_right_side + lax.ppermute(normal_right_side, "bl", swap)
     antenna_gains = solve_columns(inverse, normal_right_side)
     amplitude_gain = antenna_gains[0]
     phase_gain_term = antenna_gains[1]

time: 461 us -> 976 us (2.12)
  waiting for transfers between devices: 263 us -> 750 us
  local copies, waits for them, and re-layouts: 41 us -> 58.4 us
    ppermute x0 -> x5, waiting for transfers between devices: none -> 646 us  [on_device(): lax.ppermute(normal_right_side, 'bl', swap)]
    psum x1 -> x0, waiting for transfers between devices: 161 us -> none  [on_device(): normal_right_side = lax.psum(rhs_part, 'bl')]
    add x0 -> x4, local copies, waits for them, and re-layouts: none -> 15.3 us  [on_device(): normal_right_side + lax.ppermute(normal_right_side, 'bl', swap)]
  transfers between devices with their start and end apart: 3 -> 7, of which waited for: 3 -> 7; matrix products, arithmetic and copies ran while one was open for 3% -> 1% of each run, Pallas kernels for 0% -> 0%
where the time goes in v1:
time: 976 us; the launch traced here: 966 us
  waiting for transfers between devices  750 us (77%)
  blocking collectives  64.7 us (7%)
  local copies, waits for them, and re-layouts  58.4 us (6%)
  matrix products  46.5 us (5%)
  other arithmetic  17.7 us (2%)
  between operations  14.8 us (2%)
  starting transfers between devices  14.5 us (1%)
    ppermute x5, waiting for transfers between devices, on_device(): lax.ppermute(normal_right_side, 'bl', swap)  646 us
    psum x1, waiting for transfers between devices, on_device(): group_sums, group_counts = lax.psum((group_part, count_part), 'bl')  93.2 us
    psum x1, blocking collectives, on_device(): group_sums, group_counts = lax.psum((group_part, count_part), 'bl')  64.7 us
  transfers between devices with their start and end apart: 7, of which 7 were waited for; matrix products, arithmetic and copies ran while one was open for 1% of the time, Pallas kernels for 0%

profile of v1, /device:TPU:1, one launch (start us, length us, event | category | flops | bytes accessed | tf_op | source)
XLA Modules:
  0.0 966.2 jit_solution(12369519201613334938)
XLA Ops:
  7.2 3.5 convolution_bitcast_fusion.1
  10.9 64.7 %psum.15 = f32[224]{0:T(256)S(1)} all-reduce(f32[224]{0:T(256)S(1)} %convert_reduce_fusion), channel_id=1, replica_groups=mesh['bl'=32,'ta'=8] {'bl'}, use_global_device_ids=true, to_apply=%region_2.0 | all-reduce | flops 224 | bytes 1792 | tf_op jit(solution)/shard_map/psum | solution.py:69
  75.7 93.2 %all-reduce.4.cloned.1.call-done = f32[2,224,1,1536]{3,1,0,2:T(8,128)} async-done(((f32[2,224,1,1536]{3,1,0,2:T(8,128)}), f32[2,224,1,1536]{3,1,0,2:T(8,128)}) %all-reduce.4.cloned.1.call-update) | async-done | bytes 2752528 | tf_op jit(solution)/shard_map/psum | solution.py:69
  168.9 2.1 divide_bitcast_fusion
  171.0 3.7 copy.75
  174.6 7.3 gather_fusion
  181.9 6.4 convolution_bitcast_fusion
  188.4 3.5 copy.77
  191.9 0.6 collective-permute-start
  192.5 89.6 %collective-permute-done = f32[2,350,1,1536]{3,0,2,1:T(2,128)S(1)} collective-permute-done((f32[2,350,1,1536]{3,0,2,1:T(2,128)S(1)}, f32[2,350,1,1536]{3,0,2,1:T(2,128)S(1)}, u32[]{:S(2)}, u32[]{:S(2)}) %collective-permute-start) | collective-permute-done | bytes 4300832 | tf_op jit(solution)/shard_map/ppermute | solution.py:80
  282.1 1.1 copy_add_fusion.5
  283.2 3.3 copy.79
  286.5 1.1 collective-permute-start.1
  287.6 186.7 %collective-permute-done.1 = f32[2,350,1,1536]{3,0,2,1:T(2,128)S(1)} collective-permute-done((f32[2,350,1,1536]{3,0,2,1:T(2,128)S(1)}, f32[2,350,1,1536]{3,0,2,1:T(2,128)S(1)}, u32[]{:S(2)}, u32[]{:S(2)}) %collective-permute-start.1) | collective-permute-done | bytes 4300832 | tf_op jit(solution)/shard_map/ppermute | solution.py:80
  474.3 1.1 copy_add_fusion.4
  475.4 3.3 copy.81
  478.8 0.7 collective-permute-start.2
  479.4 187.4 %collective-permute-done.2 = f32[2,350,1,1536]{3,0,2,1:T(2,128)S(1)} collective-permute-done((f32[2,350,1,1536]{3,0,2,1:T(2,128)S(1)}, f32[2,350,1,1536]{3,0,2,1:T(2,128)S(1)}, u32[]{:S(2)}, u32[]{:S(2)}) %collective-permute-start.2) | collective-permute-done | bytes 4300832 | tf_op jit(solution)/shard_map/ppermute | solution.py:80
  666.8 1.1 copy_add_fusion.3
  667.9 3.3 copy.83
  671.2 0.3 collective-permute-start.3
  671.5 92.8 %collective-permute-done.3 = f32[2,350,1,1536]{3,0,2,1:T(2,128)S(1)} collective-permute-done((f32[2,350,1,1536]{3,0,2,1:T(2,128)S(1)}, f32[2,350,1,1536]{3,0,2,1:T(2,128)S(1)}, u32[]{:S(2)}, u32[]{:S(2)}) %collective-permute-start.3) | collective-permute-done | bytes 4300832 | tf_op jit(solution)/shard_map/ppermute | solution.py:80
  764.2 1.1 copy_add_fusion.2
  765.4 5.4 copy.85
  770.7 4.5 collective-permute-start.4
  776.1 0.2 convolution_add_fusion.5
  777.2 89.8 %collective-permute-done.4 = f32[2,350,1,1536]{3,0,2,1:T(2,128)} collective-permute-done((f32[2,350,1,1536]{3,0,2,1:T(2,128)}, f32[2,350,1,1536]{3,0,2,1:T(2,128)}, u32[]{:S(2)}, u32[]{:S(2)}) %collective-permute-start.4) | collective-permute-done | bytes 4300832 | tf_op jit(solution)/shard_map/ppermute | solution.py:80
  867.0 9.8 %fusion = f32[2,1536,350]{1,2,0:T(8,128)S(1)} fusion(f32[2,350,1,1536]{3,1,0,2:T(8,128)} %copy-done.3, f32[2,350,1,1536]{3,0,2,1:T(2,128)} %collective-permute-done.4, f32[2,350,350]{2,0,1:T(2,128)S(1)} %copy-done), kind=kOutput, calls=%fused_computation.5 | convolution fusion | flops 4516915200 | bytes 13882400 | tf_op jit(solution)/shard_map/sab,sbtf->satf/dot_general | solution.py:42
  876.9 1.8 slice_bitcast_fusion.1
  878.7 0.8 copy-done.2
  879.6 4.7 gather_fusion.2
  884.3 4.7 gather_fusion.1
  889.0 2.3 gather_fusion.3
  891.3 2.3 gather_fusion.4
  893.7 9.3 fusion.31
  903.2 2.8 copy.89
  905.9 7.3 all-to-all-start
  913.4 1.4 broadcast_multiply_fusion
  914.8 8.7 copy.94
  923.6 10.2 %all-to-all-done = bf16[2,256,1,1536]{3,0,2,1:T(2,128)(2,1)S(1)} async-done(((bf16[2,256,1,1536]{3,0,2,1:T(2,128)(2,1)}), bf16[2,256,1,1536]{3,0,2,1:T(2,128)(2,1)S(1)}, u32[]{:S(2)}, u32[]{:S(2)}) %all-to-all-start) | async-done | bytes 1572896 | tf_op jit(solution)/shard_map/all_to_all | solution.py:99
  933.8 1.1 fusion.19
  934.8 1.1 fusion.60
  935.9 1.2 fusion.58
  937.1 1.2 fusion.56
  938.3 2.9 fusion.53
  941.3 2.9 fusion.51
  944.1 3.0 fusion.49
  947.1 11.8 %fusion.3 = f32[2,32,8,1536]{3,2,1,0:T(8,128)} fusion(f32[2,32,8,12,128]{4,2,3,1,0:T(8,128)} %fusion.49, f32[2,32,8,12,128]{4,2,3,1,0:T(8,128)} %fusion.51, f32[2,32,8,12,128]{4,2,3,1,0:T(8,128)} %fusion.53, f32[2,32,8,12,128]{4,2,3,1,0:T(8,128)S(1)} %fusion.19, f32[2,32,8,12,128]{4,2,3,1,0:T(8,128)S(1)} %fusion.56, f32[2,32,8,12,128]{4,2,3,1,0:T(8,128)S(1)} %fusion.60, ...), kind=kOutput, calls=%fused_computation.16 | convolution fusion | flops 84148224 | bytes 28705024 | tf_op jit(solution)/shard_map/tu,kbuf->kbtf/dot_general | solution.py:32
  (54 shorter events, 2.3 us)
Async XLA Ops:
  7.2 859.9 %copy-start = (f32[2,350,350]{2,0,1:T(2,128)S(1)}, f32[2,350,350]{2,0,1:T(2,128)}, u32[]{:S(2)}) copy-start(f32[2,350,350]{2,0,1:T(2,128)} %param.15) | copy-start | bytes 2940004
  7.2 161.7 %all-reduce.4.cloned.1.call-start = ((), (), s32[]{:S(2)}) async-start(), calls=%async_computation.1 | async-start | bytes 5505024 | tf_op jit(solution)/shard_map/psum | solution.py:69
  7.2 3.6 copy-start.11
  7.2 68.4 %copy-start.13 = (s32[256,2]{0,1:T(2,128)S(1)}, s32[256,2]{0,1:T(2,128)}, u32[]{:S(2)}) copy-start(s32[256,2]{0,1:T(2,128)} %param.13) | copy-start | bytes 6148
  174.6 7.3 copy-start.5
  174.6 7.3 copy-start.7
  191.9 90.2 %collective-permute-start = (f32[2,350,1,1536]{3,0,2,1:T(2,128)S(1)}, f32[2,350,1,1536]{3,0,2,1:T(2,128)S(1)}, u32[]{:S(2)}, u32[]{:S(2)}) collective-permute-start(f32[2,350,1,1536]{3,0,2,1:T(2,128)S(1)} %copy.77), channel_id=1, source_target_pairs={{0,8},{8,0},{16,24},{24,16},{32,40},{40,32},{48,56},{56,48},{64,72... | collective-permute-start | bytes 12902408 | tf_op jit(solution)/shard_map/ppermute | solution.py:80
  286.5 187.8 %collective-permute-start.1 = (f32[2,350,1,1536]{3,0,2,1:T(2,128)S(1)}, f32[2,350,1,1536]{3,0,2,1:T(2,128)S(1)}, u32[]{:S(2)}, u32[]{:S(2)}) collective-permute-start(f32[2,350,1,1536]{3,0,2,1:T(2,128)S(1)} %copy.79), channel_id=1, source_target_pairs={{0,16},{8,24},{16,0},{24,8},{32,48},{40,56},{48,32},{56,40},{64,80... | collective-permute-start | bytes 12902408 | tf_op jit(solution)/shard_map/ppermute | solution.py:80
  478.8 188.0 %collective-permute-start.2 = (f32[2,350,1,1536]{3,0,2,1:T(2,128)S(1)}, f32[2,350,1,1536]{3,0,2,1:T(2,128)S(1)}, u32[]{:S(2)}, u32[]{:S(2)}) collective-permute-start(f32[2,350,1,1536]{3,0,2,1:T(2,128)S(1)} %copy.81), channel_id=1, source_target_pairs={{0,32},{8,40},{16,48},{24,56},{32,0},{40,8},{48,16},{56,24},{64,96... | collective-permute-start | bytes 12902408 | tf_op jit(solution)/shard_map/ppermute | solution.py:80
  671.2 93.0 %collective-permute-start.3 = (f32[2,350,1,1536]{3,0,2,1:T(2,128)S(1)}, f32[2,350,1,1536]{3,0,2,1:T(2,128)S(1)}, u32[]{:S(2)}, u32[]{:S(2)}) collective-permute-start(f32[2,350,1,1536]{3,0,2,1:T(2,128)S(1)} %copy.83), channel_id=1, source_target_pairs={{0,64},{8,72},{16,80},{24,88},{32,96},{40,104},{48,112},{56,120},{... | collective-permute-start | bytes 12902408 | tf_op jit(solution)/shard_map/ppermute | solution.py:80
  765.3 5.4 copy-start.3
  765.3 9.9 %copy-start.12 = (s32[32,12]{0,1:T(8,128)S(1)}, s32[32,12]{0,1:T(8,128)}, u32[]{:S(2)}) copy-start(s32[32,12]{0,1:T(8,128)} %param.14) | copy-start | bytes 4612
  765.4 10.0 %copy-start.8 = (bf16[7,128,128]{2,1,0:T(8,128)(2,1)S(1)}, bf16[7,128,128]{2,1,0:T(8,128)(2,1)}, u32[]{:S(2)}) copy-start(bf16[7,128,128]{2,1,0:T(8,128)(2,1)} %param.17) | copy-start | bytes 688132
  770.7 6.3 copy-start.10
  770.7 96.3 %collective-permute-start.4 = (f32[2,350,1,1536]{3,0,2,1:T(2,128)}, f32[2,350,1,1536]{3,0,2,1:T(2,128)}, u32[]{:S(2)}, u32[]{:S(2)}) collective-permute-start(f32[2,350,1,1536]{3,0,2,1:T(2,128)} %copy.85), channel_id=1, source_target_pairs={{0,128},{8,136},{16,144},{24,152},{32,160},{40,168},{48,176},{56,1... | collective-permute-start | bytes 12902408 | tf_op jit(solution)/shard_map/ppermute | solution.py:80
  876.9 2.7 copy-start.2
  891.3 2.3 copy-start.6
  905.9 27.8 %all-to-all-start = ((bf16[2,256,1,1536]{3,0,2,1:T(2,128)(2,1)}), bf16[2,256,1,1536]{3,0,2,1:T(2,128)(2,1)S(1)}, u32[]{:S(2)}, u32[]{:S(2)}) async-start(bf16[2,256,1,1536]{3,0,2,1:T(2,128)(2,1)} %copy.89), calls=%async_computation | async-start | bytes 3145728 | tf_op jit(solution)/shard_map/all_to_all | solution.py:99
  914.8 18.9 %copy-start.9 = (bf16[7,128,128]{2,1,0:T(8,128)(2,1)S(1)}, bf16[7,128,128]{2,1,0:T(8,128)(2,1)}, u32[]{:S(2)}) copy-start(bf16[7,128,128]{2,1,0:T(8,128)(2,1)} %param.17) | copy-start | bytes 688132
  944.1 3.0 copy-start.4
  947.1 11.8 %copy-start.1 = (f32[2,350,350]{2,0,1:T(2,128)S(1)}, f32[2,350,350]{2,0,1:T(2,128)}, u32[]{:S(2)}) copy-start(f32[2,350,350]{2,0,1:T(2,128)} %param.15) | copy-start | bytes 2940004
Sparse Core Ops, SparseCore 0:
  12.1 156.7 all-reduce.3
